TPU v7x, 128 devices: a whole 4x4x4 slice. The times are simulated.
128 devices in a mesh: energy: 8 (over y, core), layer: 16 (over x, z).
Axes of the slice: x: 4, y: 4, z: 4, core: 2. Of those that a mesh axis runs over, the one named last changes fastest.
Arguments:
- correlations: bfloat16 [128, 16, 4, 256, 256], P(('energy', 'layer')), may hold values from -6 to 6
- retarded: bfloat16 [128, 16, 2, 256, 256], P(('energy', 'layer')), may hold values from -0.15625 to 0.15625
- coupling: bfloat16 [16, 256, 256], P('layer'), may hold values from -0.375 to 0.375
- phonon_shifts: int32 [4], replicated, may hold values from 1 to 4, as said below
- phonon_coupling: float32 [4], replicated, may hold values from 0.3 to 1.2
- layer_orbitals: int32 [16], P('layer'), may hold values from 128 to 256, as said below
Outputs:
- left_correlations: bfloat16 [128, 16, 4, 256, 256], P('energy', 'layer')
Inputs may be any that keep to these rules, and one draw needn't show every extreme that they name: `phonon_shifts`: one of the offsets equals 4. `layer_orbitals`: some layer has all 256 orbitals live.
All inputs are finite; a program needn't handle non-finite values.
Results may differ from a plain program's by a relative error of at most 0.025.
Values may be sent and summed in bfloat16 or wider, within the bound.
No kernel may reach another device: no remote copies, remote signals or barrier semaphores. Data moves between devices by JAX's collectives and lax.ppermute only.
A program may use at most 128 MiB of HBM per device.

v0:
```python
import jax
import jax.numpy as jnp
from jax import lax
from jax.sharding import PartitionSpec as P

MODES = 4
SHIFT_MAX = 4
bose_ratio = 0.5


def with_halo(block, sides, width):
    for axis, dim in sides:
        count = lax.axis_size(axis)
        forward = [(i, i + 1) for i in range(count - 1)]
        backward = [(target, source) for source, target in forward]
        low = lax.ppermute(
            lax.slice_in_dim(block, block.shape[dim] - width, None, axis=dim), axis, forward
        )
        high = lax.ppermute(lax.slice_in_dim(block, 0, width, axis=dim), axis, backward)
        block = jnp.concatenate([low, block, high], axis=dim)
    return block


def mode_weights(shift_value):
    occupation = 1.0 / (jnp.exp(bose_ratio * shift_value.astype(jnp.float32)) - 1.0)
    lower_weight = jnp.stack([occupation, occupation, occupation + 1.0, occupation + 1.0])
    upper_weight = jnp.stack([occupation + 1.0, occupation + 1.0, occupation, occupation])
    return (lower_weight, upper_weight)


def left_product(matrix, stacked_block):
    return jnp.einsum(
        "...ab,...kbc->...kac", matrix, stacked_block, preferred_element_type=jnp.float32
    )


def right_product(stacked_block, matrix):
    return jnp.einsum(
        "...kab,...cb->...kac", stacked_block, matrix, preferred_element_type=jnp.float32
    )


def advance(previous, sigma_block, green_block, coupling_block):
    halfway = jnp.einsum(
        "...kab,cb->...kac", previous, coupling_block, preferred_element_type=jnp.float32
    ).astype(jnp.bfloat16)
    spread = jnp.einsum(
        "ab,...kbc->...kac", coupling_block, halfway, preferred_element_type=jnp.float32
    )
    source = (sigma_block.astype(jnp.float32) + spread).astype(jnp.bfloat16)
    green_real = green_block[..., 0, :, :]
    green_imag = green_block[..., 1, :, :]
    source_real = source[..., 0::2, :, :]
    source_imag = source[..., 1::2, :, :]
    inner_real = (
        left_product(green_real, source_real) - left_product(green_imag, source_imag)
    ).astype(jnp.bfloat16)
    inner_imag = (
        left_product(green_real, source_imag) + left_product(green_imag, source_real)
    ).astype(jnp.bfloat16)
    outer_real = right_product(inner_real, green_real) + right_product(inner_imag, green_imag)
    outer_imag = right_product(inner_imag, green_real) - right_product(inner_real, green_imag)
    stacked = jnp.stack([outer_real, outer_imag], axis=-3)
    return stacked.reshape(stacked.shape[:-4] + (4,) + stacked.shape[-2:]).astype(jnp.bfloat16)


def body(correlations, retarded, coupling, phonon_shifts, phonon_coupling, layer_orbitals):
    regrouped = lax.all_to_all(correlations, "layer", split_axis=1, concat_axis=0, tiled=True)
    energies_here = regrouped.shape[0]
    orbital_count = regrouped.shape[-1]
    padded = with_halo(regrouped, (("energy", 0),), SHIFT_MAX)
    accumulated = jnp.zeros(regrouped.shape, jnp.float32)
    for mode_index in range(MODES):
        shift_value = phonon_shifts[mode_index]
        lower_weight, upper_weight = mode_weights(shift_value)
        lower_block = lax.dynamic_slice_in_dim(padded, SHIFT_MAX - shift_value, energies_here, 0)
        upper_block = lax.dynamic_slice_in_dim(padded, SHIFT_MAX + shift_value, energies_here, 0)
        accumulated = accumulated + phonon_coupling[mode_index] * (
            lower_weight[:, None, None] * lower_block.astype(jnp.float32)
            + upper_weight[:, None, None] * upper_block.astype(jnp.float32)
        )
    orbital_index = jnp.arange(orbital_count, dtype=jnp.int32)
    live_count = layer_orbitals[:, None, None, None]
    live_mask = (orbital_index[:, None] < live_count) & (orbital_index[None, :] < live_count)
    sigma_blocks = jnp.where(live_mask, accumulated, 0.0).astype(jnp.bfloat16)
    returned = lax.all_to_all(sigma_blocks, "layer", split_axis=0, concat_axis=1, tiled=True)
    couplings = lax.all_gather(coupling, "layer", axis=0, tiled=True)
    layer_total = returned.shape[1]

    def layer_step(layer_index, state):
        previous, finished = state
        current = advance(
            previous,
            lax.dynamic_index_in_dim(returned, layer_index, 1, keepdims=False),
            lax.dynamic_index_in_dim(retarded, layer_index, 1, keepdims=False),
            lax.dynamic_index_in_dim(couplings, layer_index, 0, keepdims=False),
        )
        finished = lax.dynamic_update_index_in_dim(finished, current, layer_index, 1)
        return (current, finished)

    _, finished = lax.fori_loop(
        0, layer_total, layer_step, (correlations[:, 0], jnp.zeros_like(correlations))
    )
    return lax.all_to_all(finished, "layer", split_axis=1, concat_axis=0, tiled=True)


def solution(mesh):
    return jax.shard_map(
        body,
        mesh=mesh,
        in_specs=(
            P(("energy", "layer"), None, None, None, None),
            P(("energy", "layer"), None, None, None, None),
            P("layer", None, None),
            P(),
            P(),
            P("layer"),
        ),
        out_specs=P("energy", "layer", None, None, None),
        check_vma=False,
    )
```

profile of v0, /device:TPU:8, one launch (start us, length us, event | category | flops | bytes accessed | tf_op | source)
XLA Modules:
  0.0 559.1 jit_solution(11851508432102478930)
XLA Ops:
  6.5 12.2 %copy.25 = bf16[1,16,4,256,256]{3,4,2,0,1:T(8,128)(2,1)} copy(bf16[1,16,4,256,256]{4,3,2,1,0:T(8,128)(2,1)} %param.8) | data formatting | bytes 16777216 | tf_op args[0]
  18.8 104.3 %all_to_all.39 = bf16[1,16,4,256,256]{3,4,2,0,1:T(8,128)(2,1)S(1)} all-to-all(bf16[1,16,4,256,256]{3,4,2,0,1:T(8,128)(2,1)} %copy.25), channel_id=1, replica_groups=mesh['energy'=8,'layer'=16] {'layer'}, dimensions={1} | all-to-all | bytes 16777216 | tf_op jit(solution)/shard_map/all_to_all | solution.py:68
  123.1 1.6 slice_bitcast_fusion.11
  124.7 2.4 copy-done
  127.1 1.5 slice_bitcast_fusion.10
  128.6 1.9 collective-permute-start.1
  130.6 2.4 collective-permute-start
  148.3 6.1 %collective-permute-done.1 = bf16[4,1,4,256,256]{3,4,2,0,1:T(8,128)(2,1)S(1)} collective-permute-done((bf16[4,1,4,256,256]{3,4,2,0,1:T(8,128)(2,1)}, bf16[4,1,4,256,256]{3,4,2,0,1:T(8,128)(2,1)S(1)}, u32[]{:S(2)}, u32[]{:S(2)}) %collective-permute-start.1) | collective-permute-done | bytes 2097184 | tf_op jit(solution)/shard_map/ppermute | solution.py:19
  154.4 3.8 collective-permute-done
  158.2 6.4 %pad_maximum_fusion = bf16[24,1,4,256,256]{3,4,2,0,1:T(8,128)(2,1)S(1)} fusion(bf16[4,1,4,256,256]{3,4,2,0,1:T(8,128)(2,1)} %copy-done.1, bf16[16,1,4,256,256]{3,4,2,0,1:T(8,128)(2,1)} %bitcast.174, bf16[4,1,4,256,256]{3,4,2,0,1:T(8,128)(2,1)} %collective-permute-done), kind=kLoop, calls=%fused_computation.37 | loop fusion | flops 12582912 | bytes 25165824 | tf_op jit(solution)/shard_map/concatenate | solution.py:20
  164.6 20.0 %fusion.29 = bf16[16,1,4,256,256]{3,4,2,1,0:T(8,128)(2,1)} fusion(bf16[24,1,4,256,256]{3,4,2,0,1:T(8,128)(2,1)S(1)} %pad_maximum_fusion, s32[]{:T(128)S(6)} %select_n.47, f32[4]{0:T(128)S(1)} %get-tuple-element.136, s32[]{:T(128)S(6)} %select_n.46, f32[4]{0:T(128)S(1)} %get-tuple-element.135, f32[]{:T(128)} %bitcast.51, s32[]{:T(128)S(6)} %select_n.45, ...), kind=kLoop, calls=%fused_computation.38 | loop fusion | flops 121634816 | bytes 75563184 | tf_op jit(solution)/shard_map/convert_element_type | solution.py:85
  184.6 4.7 all-to-all-start.1
  190.1 1.1 slice_bitcast_fusion.12
  191.2 142.2 %all-gather.2.cloned.1.call-done = bf16[16,256,256]{2,1,0:T(8,128)(2,1)} async-done(((bf16[1,256,256]{2,1,0:T(8,128)(2,1)}), bf16[16,256,256]{2,1,0:T(8,128)(2,1)}) %all-gather.2.cloned.1.call-update) | async-done | bytes 2097168 | tf_op jit(solution)/shard_map/all_gather | solution.py:87
  333.4 6.0 %all-to-all-done.1 = bf16[16,1,4,256,256]{3,4,2,1,0:T(8,128)(2,1)} async-done(((bf16[16,1,4,256,256]{3,4,2,1,0:T(8,128)(2,1)}), bf16[16,1,4,256,256]{3,4,2,1,0:T(8,128)(2,1)}, u32[]{:S(2)}, u32[]{:S(2)}) %all-to-all-start.1) | async-done | bytes 8388640 | tf_op jit(solution)/shard_map/all_to_all | solution.py:86
  339.3 92.7 %while.15 = (s32[]{:T(128)}, bf16[1,4,256,256]{3,2,1,0:T(8,128)(2,1)S(1)}, bf16[1,16,4,256,256]{4,3,2,1,0:T(8,128)(2,1)}, bf16[1,16,4,256,256]{3,4,2,1,0:T(8,128...) while((s32[]{:T(128)}, ...), condition=%wide.region_1.2_spmd, body=%wide.region_0.1_spmd.sunk | while | flops 807665664 | bytes 13895261 | solution.py:101
  339.3 1.0 dynamic-slice_bitcast_fusion.2
  340.3 1.7 fusion.67
  344.3 0.8 bitcast_dynamic-update-slice_fusion.2
  345.1 1.0 dynamic-slice_bitcast_fusion.2
  346.1 1.7 fusion.67
  350.1 0.8 bitcast_dynamic-update-slice_fusion.2
  350.9 1.0 dynamic-slice_bitcast_fusion.2
  351.9 1.7 fusion.67
  355.9 0.8 bitcast_dynamic-update-slice_fusion.2
  356.7 1.0 dynamic-slice_bitcast_fusion.2
  357.7 1.7 fusion.67
  361.7 0.8 bitcast_dynamic-update-slice_fusion.2
  362.5 1.0 dynamic-slice_bitcast_fusion.2
  363.5 1.7 fusion.67
  368.3 1.0 dynamic-slice_bitcast_fusion.2
  369.3 1.7 fusion.67
  373.3 0.8 bitcast_dynamic-update-slice_fusion.2
  374.1 1.0 dynamic-slice_bitcast_fusion.2
  375.1 1.7 fusion.67
  379.1 0.8 bitcast_dynamic-update-slice_fusion.2
  379.9 1.0 dynamic-slice_bitcast_fusion.2
  380.9 1.7 fusion.67
  384.9 0.8 bitcast_dynamic-update-slice_fusion.2
  385.7 1.0 dynamic-slice_bitcast_fusion.2
  386.7 1.7 fusion.67
  390.7 0.8 bitcast_dynamic-update-slice_fusion.2
  391.5 1.0 dynamic-slice_bitcast_fusion.2
  392.5 1.7 fusion.67
  396.5 0.8 bitcast_dynamic-update-slice_fusion.2
  397.3 1.0 dynamic-slice_bitcast_fusion.2
  398.3 1.7 fusion.67
  402.2 0.8 bitcast_dynamic-update-slice_fusion.2
  403.1 1.0 dynamic-slice_bitcast_fusion.2
  404.0 1.7 fusion.67
  408.0 0.8 bitcast_dynamic-update-slice_fusion.2
  408.9 1.0 dynamic-slice_bitcast_fusion.2
  409.8 1.7 fusion.67
  413.8 0.8 bitcast_dynamic-update-slice_fusion.2
  414.7 1.0 dynamic-slice_bitcast_fusion.2
  415.6 1.7 fusion.67
  419.6 0.8 bitcast_dynamic-update-slice_fusion.2
  420.5 1.0 dynamic-slice_bitcast_fusion.2
  421.4 1.7 fusion.67
  425.4 0.8 bitcast_dynamic-update-slice_fusion.2
  426.3 1.0 dynamic-slice_bitcast_fusion.2
  427.2 1.7 fusion.67
  432.0 112.4 %all_to_all.40 = bf16[1,16,4,256,256]{4,3,2,0,1:T(8,128)(2,1)} all-to-all(bf16[1,16,4,256,256]{4,3,2,0,1:T(8,128)(2,1)} %bitcast.176), channel_id=1, replica_groups=mesh['energy'=8,'layer'=16] {'layer'}, dimensions={1} | all-to-all | bytes 16777216 | tf_op jit(solution)/shard_map/all_to_all | solution.py:104
  544.4 7.8 %copy.49 = bf16[16,1,4,256,256]{4,3,2,1,0:T(8,128)(2,1)} copy(bf16[16,1,4,256,256]{4,3,2,1,0:T(8,128)(2,1)} %bitcast.175) | data formatting | bytes 16777216
  (180 shorter events, 39.6 us)
Async XLA Ops:
  18.8 114.2 %copy-start.2 = (s32[4]{0:T(128)S(1)}, s32[4]{0:T(128)}, u32[]{:S(2)}) copy-start(s32[4]{0:T(128)} %param.11) | copy-start | bytes 52
  18.8 128.8 %copy-start.3 = (f32[4]{0:T(128)S(1)}, f32[4]{0:T(128)}, u32[]{:S(2)}) copy-start(f32[4]{0:T(128)} %param.12) | copy-start | bytes 52
  123.1 4.0 copy-start
  128.6 25.8 %collective-permute-start.1 = (bf16[4,1,4,256,256]{3,4,2,0,1:T(8,128)(2,1)}, bf16[4,1,4,256,256]{3,4,2,0,1:T(8,128)(2,1)S(1)}, u32[]{:S(2)}, u32[]{:S(2)}) collective-permute-start(bf16[4,1,4,256,256]{3,4,2,0,1:T(8,128)(2,1)} %slice_bitcast_fusion.10), channel_id=1, source_target_pairs={{16,0},{32,16},{48,32},{64,48},{80,64},{96,80},{112,96},{17,1},{33... | collective-permute-start | bytes 6291464 | tf_op jit(solution)/shard_map/ppermute | solution.py:19
  130.6 27.7 %collective-permute-start = (bf16[4,1,4,256,256]{3,4,2,0,1:T(8,128)(2,1)}, bf16[4,1,4,256,256]{3,4,2,0,1:T(8,128)(2,1)}, u32[]{:S(2)}, u32[]{:S(2)}) collective-permute-start(bf16[4,1,4,256,256]{3,4,2,0,1:T(8,128)(2,1)} %slice_bitcast_fusion.11), channel_id=1, source_target_pairs={{0,16},{16,32},{32,48},{48,64},{64,80},{80,96},{96,112},{1,17},{17... | collective-permute-start | bytes 6291464 | tf_op jit(solution)/shard_map/ppermute | solution.py:16
  154.4 3.8 copy-start.1
  184.6 154.7 %all-to-all-start.1 = ((bf16[16,1,4,256,256]{3,4,2,1,0:T(8,128)(2,1)}), bf16[16,1,4,256,256]{3,4,2,1,0:T(8,128)(2,1)}, u32[]{:S(2)}, u32[]{:S(2)}) async-start(bf16[16,1,4,256,256]{3,4,2,1,0:T(8,128)(2,1)} %fusion.29), calls=%async_computation.1 | async-start | bytes 16777216 | tf_op jit(solution)/shard_map/all_to_all | solution.py:86
  189.4 144.0 %all-gather.2.cloned.1.call-start = ((), (), s32[]{:S(2)}) async-start(), calls=%async_computation.3 | async-start | bytes 2228224 | tf_op jit(solution)/shard_map/all_gather | solution.py:87
Sparse Core Ops, SparseCore 0:
  192.3 140.9 all-gather.1
where the time goes:
time: 561 us; the launch traced here: 559 us
  blocking collectives  217 us (39%)
  waiting for transfers between devices  159 us (28%)
  matrix products  61.4 us (11%)
  local copies, waits for them, and re-layouts  57.3 us (10%)
  other arithmetic  27.6 us (5%)
  between operations  27 us (5%)
  starting transfers between devices  9.1 us (2%)
    all_gather x1, waiting for transfers between devices, body(): couplings = lax.all_gather(coupling, 'layer', axis=0, tiled=True)  142 us
    all_to_all x1, blocking collectives, body(): lax.all_to_all(finished, 'layer', split_axis=1, concat_axis=0, tiled=True)  112 us
    all_to_all x1, blocking collectives, body(): lax.all_to_all(correlations, 'layer', split_axis=1, concat_axis=0, tiled=...  104 us
    dot_general x16, matrix products, advance(): jnp.einsum('ab,...kbc->...kac', coupling_block, halfway, preferred_elemen...  27.3 us
    unnamed x10, local copies, waits for them, and re-layouts  22.5 us
    convert_element_type x1, other arithmetic, body(): sigma_blocks = jnp.where(live_mask, accumulated, 0.0).astype(jnp.bfloat16)  20 us
    dot_general x64, matrix products, right_product(): jnp.einsum('...kab,...cb->...kac', stacked_block, matrix, preferred_eleme...  17.5 us
    dot_general x64, matrix products, left_product(): jnp.einsum('...ab,...kbc->...kac', matrix, stacked_block, preferred_eleme...  16.5 us
  transfers between devices with their start and end apart: 4, of which 4 were waited for; matrix products, arithmetic and copies ran while one was open for 1% of the time, Pallas kernels for 0%

commit v1 on v0

--- a/solution.py
+++ b/solution.py
@@ -6,6 +6,15 @@
 MODES = 4
 SHIFT_MAX = 4
 bose_ratio = 0.5
+
+
+def unite_the_shelves(field_in, across):
+    log = []
+    for _ in range(lax.axis_size(across)):
+        log.append(field_in)
+    after = lax.all_to_all(jnp.stack(log), across, 0, 0)
+    value_now = jnp.concatenate(after, 0)
+    return value_now
 
 
 def with_halo(block, sides, width):
@@ -84,7 +93,7 @@
     live_mask = (orbital_index[:, None] < live_count) & (orbital_index[None, :] < live_count)
     sigma_blocks = jnp.where(live_mask, accumulated, 0.0).astype(jnp.bfloat16)
     returned = lax.all_to_all(sigma_blocks, "layer", split_axis=0, concat_axis=1, tiled=True)
-    couplings = lax.all_gather(coupling, "layer", axis=0, tiled=True)
+    couplings = unite_the_shelves(coupling, "layer")
     layer_total = returned.shape[1]
 
     def layer_step(layer_index, state):

time: 561 us -> 542 us (0.966)
  between operations: 27 us -> 13.6 us
  blocking collectives: 217 us -> 208 us
    all_to_all x1, waiting for transfers between devices: 5.97 us -> 152 us  [body(): lax.all_to_all(sigma_blocks, 'layer', split_axis=0, concat_axis=1, tiled=...]
    all_gather x1 -> x0, waiting for transfers between devices: 142 us -> none  [body(): couplings = lax.all_gather(coupling, 'layer', axis=0, tiled=True)]
    all_to_all x1, blocking collectives: 112 us -> 104 us  [body(): lax.all_to_all(finished, 'layer', split_axis=1, concat_axis=0, tiled=True)]
    ppermute x1, waiting for transfers between devices: 6.13 us -> 0.15 us  [with_halo(): lax.ppermute(lax.slice_in_dim(block, 0, width, axis=dim), axis, backward)]
    unnamed x10 -> x12, local copies, waits for them, and re-layouts: 22.5 us -> 22.5 us
  transfers between devices with their start and end apart: 4 -> 4, of which waited for: 4 -> 3; matrix products, arithmetic and copies ran while one was open for 1% -> 6% of each run, Pallas kernels for 0% -> 0%
where the time goes in v1:
time: 542 us; the launch traced here: 540 us
  blocking collectives  208 us (38%)
  waiting for transfers between devices  156 us (29%)
  matrix products  61.4 us (11%)
  local copies, waits for them, and re-layouts  58.9 us (11%)
  other arithmetic  27.8 us (5%)
  between operations  13.6 us (3%)
  starting transfers between devices  13.5 us (2%)
    all_to_all x1, waiting for transfers between devices, body(): lax.all_to_all(sigma_blocks, 'layer', split_axis=0, concat_axis=1, tiled=...  152 us
    all_to_all x1, blocking collectives, body(): lax.all_to_all(correlations, 'layer', split_axis=1, concat_axis=0, tiled=...  104 us
    all_to_all x1, blocking collectives, body(): lax.all_to_all(finished, 'layer', split_axis=1, concat_axis=0, tiled=True)  104 us
    dot_general x16, matrix products, advance(): jnp.einsum('ab,...kbc->...kac', coupling_block, halfway, preferred_elemen...  27.3 us
    unnamed x12, local copies, waits for them, and re-layouts  22.5 us
    convert_element_type x1, other arithmetic, body(): sigma_blocks = jnp.where(live_mask, accumulated, 0.0).astype(jnp.bfloat16)  20.1 us
    dot_general x64, matrix products, right_product(): jnp.einsum('...kab,...cb->...kac', stacked_block, matrix, preferred_eleme...  17.5 us
    dot_general x64, matrix products, left_product(): jnp.einsum('...ab,...kbc->...kac', matrix, stacked_block, preferred_eleme...  16.5 us
  transfers between devices with their start and end apart: 4, of which 3 were waited for; matrix products, arithmetic and copies ran while one was open for 6% of the time, Pallas kernels for 0%

profile of v1, /device:TPU:8, one launch (start us, length us, event | category | flops | bytes accessed | tf_op | source)
XLA Modules:
  0.0 540.4 jit_solution(3757865576755807672)
XLA Ops:
  0.0 12.2 %copy.25 = bf16[1,16,4,256,256]{3,4,2,0,1:T(8,128)(2,1)} copy(bf16[1,16,4,256,256]{4,3,2,1,0:T(8,128)(2,1)} %param.8) | data formatting | bytes 16777216 | tf_op args[0]
  12.2 104.3 %all_to_all.44 = bf16[1,16,4,256,256]{3,4,2,0,1:T(8,128)(2,1)S(1)} all-to-all(bf16[1,16,4,256,256]{3,4,2,0,1:T(8,128)(2,1)} %copy.25), channel_id=1, replica_groups=mesh['energy'=8,'layer'=16] {'layer'}, dimensions={1} | all-to-all | bytes 16777216 | tf_op jit(solution)/shard_map/all_to_all | solution.py:77
  116.6 1.6 slice_bitcast_fusion.11
  118.2 2.4 copy-done
  120.6 1.5 slice_bitcast_fusion.10
  122.1 1.9 collective-permute-start.1
  124.0 2.4 collective-permute-start
  126.5 1.5 stack.128
  128.0 4.4 all-to-all-start.2
  147.9 3.8 collective-permute-done
  151.7 6.4 %pad_maximum_fusion = bf16[24,1,4,256,256]{3,4,2,0,1:T(8,128)(2,1)S(1)} fusion(bf16[4,1,4,256,256]{3,4,2,0,1:T(8,128)(2,1)} %copy-done.1, bf16[16,1,4,256,256]{3,4,2,0,1:T(8,128)(2,1)} %bitcast.176, bf16[4,1,4,256,256]{3,4,2,0,1:T(8,128)(2,1)} %collective-permute-done), kind=kLoop, calls=%fused_computation.37 | loop fusion | flops 12582912 | bytes 25165824 | tf_op jit(solution)/shard_map/concatenate | solution.py:29
  158.1 20.1 %fusion.29 = bf16[16,1,4,256,256]{3,4,2,1,0:T(8,128)(2,1)} fusion(bf16[24,1,4,256,256]{3,4,2,0,1:T(8,128)(2,1)S(1)} %pad_maximum_fusion, s32[]{:T(128)S(6)} %select_n.47, f32[4]{0:T(128)S(1)} %get-tuple-element.136, s32[]{:T(128)S(6)} %select_n.46, f32[4]{0:T(128)S(1)} %get-tuple-element.135, f32[]{:T(128)} %bitcast.51, s32[]{:T(128)S(6)} %select_n.45, ...), kind=kLoop, calls=%fused_computation.38 | loop fusion | flops 121634816 | bytes 75563184 | tf_op jit(solution)/shard_map/convert_element_type | solution.py:94
  178.2 4.7 all-to-all-start.1
  183.0 1.1 slice_bitcast_fusion.12
  184.1 151.9 %all-to-all-done.1 = bf16[16,1,4,256,256]{3,4,2,1,0:T(8,128)(2,1)} async-done(((bf16[16,1,4,256,256]{3,4,2,1,0:T(8,128)(2,1)}), bf16[16,1,4,256,256]{3,4,2,1,0:T(8,128)(2,1)}, u32[]{:S(2)}, u32[]{:S(2)}) %all-to-all-start.1) | async-done | bytes 8388640 | tf_op jit(solution)/shard_map/all_to_all | solution.py:95
  336.0 92.7 %while.15 = (s32[]{:T(128)}, bf16[1,4,256,256]{3,2,1,0:T(8,128)(2,1)S(1)}, bf16[1,16,4,256,256]{4,3,2,1,0:T(8,128)(2,1)}, bf16[1,16,4,256,256]{3,4,2,1,0:T(8,128...) while((s32[]{:T(128)}, ...), condition=%wide.region_1.2_spmd, body=%wide.region_0.1_spmd.sunk | while | flops 807665664 | bytes 13895261 | solution.py:110
  336.0 1.0 dynamic-slice_bitcast_fusion.2
  337.0 1.7 fusion.67
  341.0 0.8 bitcast_dynamic-update-slice_fusion.2
  341.8 1.0 dynamic-slice_bitcast_fusion.2
  342.8 1.7 fusion.67
  346.8 0.8 bitcast_dynamic-update-slice_fusion.2
  347.6 1.0 dynamic-slice_bitcast_fusion.2
  348.6 1.7 fusion.67
  352.6 0.8 bitcast_dynamic-update-slice_fusion.2
  353.4 1.0 dynamic-slice_bitcast_fusion.2
  354.4 1.7 fusion.67
  358.3 0.8 bitcast_dynamic-update-slice_fusion.2
  359.2 1.0 dynamic-slice_bitcast_fusion.2
  360.1 1.7 fusion.67
  364.1 0.8 bitcast_dynamic-update-slice_fusion.2
  365.0 1.0 dynamic-slice_bitcast_fusion.2
  365.9 1.7 fusion.67
  369.9 0.8 bitcast_dynamic-update-slice_fusion.2
  370.8 1.0 dynamic-slice_bitcast_fusion.2
  371.7 1.7 fusion.67
  375.7 0.8 bitcast_dynamic-update-slice_fusion.2
  376.6 1.0 dynamic-slice_bitcast_fusion.2
  377.5 1.7 fusion.67
  381.5 0.8 bitcast_dynamic-update-slice_fusion.2
  382.4 1.0 dynamic-slice_bitcast_fusion.2
  383.3 1.7 fusion.67
  388.1 1.0 dynamic-slice_bitcast_fusion.2
  389.1 1.7 fusion.67
  393.1 0.8 bitcast_dynamic-update-slice_fusion.2
  393.9 1.0 dynamic-slice_bitcast_fusion.2
  394.9 1.7 fusion.67
  398.9 0.8 bitcast_dynamic-update-slice_fusion.2
  399.7 1.0 dynamic-slice_bitcast_fusion.2
  400.7 1.7 fusion.67
  404.7 0.8 bitcast_dynamic-update-slice_fusion.2
  405.5 1.0 dynamic-slice_bitcast_fusion.2
  406.5 1.7 fusion.67
  410.5 0.8 bitcast_dynamic-update-slice_fusion.2
  411.3 1.0 dynamic-slice_bitcast_fusion.2
  412.3 1.7 fusion.67
  417.1 1.0 dynamic-slice_bitcast_fusion.2
  418.1 1.7 fusion.67
  422.1 0.8 bitcast_dynamic-update-slice_fusion.2
  422.9 1.0 dynamic-slice_bitcast_fusion.2
  423.9 1.7 fusion.67
  427.9 0.8 bitcast_dynamic-update-slice_fusion.2
  428.7 104.0 %all_to_all.45 = bf16[1,16,4,256,256]{4,3,2,0,1:T(8,128)(2,1)} all-to-all(bf16[1,16,4,256,256]{4,3,2,0,1:T(8,128)(2,1)} %bitcast.178), channel_id=1, replica_groups=mesh['energy'=8,'layer'=16] {'layer'}, dimensions={1} | all-to-all | bytes 16777216 | tf_op jit(solution)/shard_map/all_to_all | solution.py:113
  532.7 7.8 %copy.49 = bf16[16,1,4,256,256]{4,3,2,1,0:T(8,128)(2,1)} copy(bf16[16,1,4,256,256]{4,3,2,1,0:T(8,128)(2,1)} %bitcast.177) | data formatting | bytes 16777216
  (182 shorter events, 39.0 us)
Async XLA Ops:
  12.2 114.2 %copy-start.2 = (bf16[1,256,256]{2,1,0:T(8,128)(2,1)S(1)}, bf16[1,256,256]{2,1,0:T(8,128)(2,1)}, u32[]{:S(2)}) copy-start(bf16[1,256,256]{2,1,0:T(8,128)(2,1)} %param.10) | copy-start | bytes 393220
  12.2 120.2 %copy-start.3 = (s32[4]{0:T(128)S(1)}, s32[4]{0:T(128)}, u32[]{:S(2)}) copy-start(s32[4]{0:T(128)} %param.11) | copy-start | bytes 52
  12.2 134.7 %copy-start.4 = (f32[4]{0:T(128)S(1)}, f32[4]{0:T(128)}, u32[]{:S(2)}) copy-start(f32[4]{0:T(128)} %param.12) | copy-start | bytes 52
  116.6 4.0 copy-start
  122.1 25.8 %collective-permute-start.1 = (bf16[4,1,4,256,256]{3,4,2,0,1:T(8,128)(2,1)}, bf16[4,1,4,256,256]{3,4,2,0,1:T(8,128)(2,1)S(1)}, u32[]{:S(2)}, u32[]{:S(2)}) collective-permute-start(bf16[4,1,4,256,256]{3,4,2,0,1:T(8,128)(2,1)} %slice_bitcast_fusion.10), channel_id=1, source_target_pairs={{16,0},{32,16},{48,32},{64,48},{80,64},{96,80},{112,96},{17,1},{33... | collective-permute-start | bytes 6291464 | tf_op jit(solution)/shard_map/ppermute | solution.py:28
  124.0 27.7 %collective-permute-start = (bf16[4,1,4,256,256]{3,4,2,0,1:T(8,128)(2,1)}, bf16[4,1,4,256,256]{3,4,2,0,1:T(8,128)(2,1)}, u32[]{:S(2)}, u32[]{:S(2)}) collective-permute-start(bf16[4,1,4,256,256]{3,4,2,0,1:T(8,128)(2,1)} %slice_bitcast_fusion.11), channel_id=1, source_target_pairs={{0,16},{16,32},{32,48},{48,64},{64,80},{80,96},{96,112},{1,17},{17... | collective-permute-start | bytes 6291464 | tf_op jit(solution)/shard_map/ppermute | solution.py:25
  128.0 50.2 %all-to-all-start.2 = ((bf16[16,1,256,256]{3,2,1,0:T(8,128)(2,1)}), bf16[16,1,256,256]{3,2,1,0:T(8,128)(2,1)}, u32[]{:S(2)}, u32[]{:S(2)}) async-start(bf16[16,1,256,256]{3,2,1,0:T(8,128)(2,1)} %stack.128), calls=%async_computation.2 | async-start | bytes 4194304 | tf_op jit(solution)/shard_map/all_to_all | solution.py:15
  147.9 3.8 copy-start.1
  178.2 157.8 %all-to-all-start.1 = ((bf16[16,1,4,256,256]{3,4,2,1,0:T(8,128)(2,1)}), bf16[16,1,4,256,256]{3,4,2,1,0:T(8,128)(2,1)}, u32[]{:S(2)}, u32[]{:S(2)}) async-start(bf16[16,1,4,256,256]{3,4,2,1,0:T(8,128)(2,1)} %fusion.29), calls=%async_computation.1 | async-start | bytes 16777216 | tf_op jit(solution)/shard_map/all_to_all | solution.py:95
